TPU v7x, 512 devices: a whole 4x4x16 slice. The times are simulated.
512 devices in a mesh: dp: 8 (over y, core), place: 64 (over x, z).
Axes of the slice: x: 4, y: 4, z: 16, core: 2. Of those that a mesh axis runs over, the one named last changes fastest.
Arguments:
- tokens: bfloat16 [8, 64, 256, 2048], P('dp', 'place'), may hold values from -6 to 6
- hidden_grad: bfloat16 [8, 64, 256, 256], P('dp', 'place'), may hold values from -6 to 6
- routing: int32 [8, 64, 4, 64], P('dp', 'place'), may hold values from 0 to 63, each once within a row
- row_count: int32 [8, 64], replicated, may hold values from 1 to 256, as said below
- old_slots: int32 [64], replicated, may hold values from 0 to 15, as said below
- new_slots: int32 [64], replicated, may hold values from 0 to 15, as said below
- master: float32 [16, 2048, 512], P(None, ('dp', 'place')), may hold values from -0.125 to 0.125
- first_moment: float32 [16, 2048, 512], P(None, ('dp', 'place')), may hold values from -0.018 to 0.018
- second_moment: float32 [16, 2048, 512], P(None, ('dp', 'place')), may hold values from 1e-06 to 0.0001
Outputs:
- new_weights: bfloat16 [64, 2048, 512], P('place')
- new_master: float32 [16, 2048, 512], P(None, ('dp', 'place'))
- new_first: float32 [16, 2048, 512], P(None, ('dp', 'place'))
- new_second: float32 [16, 2048, 512], P(None, ('dp', 'place'))
Inputs may be any that keep to these rules, and one draw needn't show every extreme that they name: `old_slots`: every expert 0 .. 15 holds at least one slot. `new_slots`: every expert 0 .. 15 holds at least one slot. The first row_count[d, p] of a device's 256 row slots are live; some device is full in every draw.
All inputs are finite; a program needn't handle non-finite values.
Results may differ from a plain program's by a relative error of at most 0.001.
The roundings to bfloat16 on the way count: a program that leaves them out, or rounds other values in their place, can miss the bound.
Values may be sent and summed in bfloat16 or wider, within the bound.
No kernel may reach another device: no remote copies, remote signals or barrier semaphores. Data moves between devices by JAX's collectives and lax.ppermute only.
A program may use at most 64 MiB of HBM per device.

v0:
```python
import jax
import jax.numpy as jnp
from jax import lax
from jax.sharding import PartitionSpec as P

decay_first = 0.9
decay_second = 0.95
learn_rate = 0.001
weight_decay = 0.1
epsilon = 1e-08
step_number = 20.0


def from_everyone(x, axis):
    copies = jnp.broadcast_to(x, (lax.axis_size(axis), *x.shape))
    return lax.all_to_all(copies, axis, split_axis=0, concat_axis=0, tiled=True)


def joined_along(parts, dim):
    lengths = list(parts.shape[1:])
    lengths[dim] *= parts.shape[0]
    return jnp.moveaxis(parts, 0, dim).reshape(lengths)


def gathered_copies(x, axis, dim):
    parts = from_everyone(x, axis)
    return joined_along(parts, dim)


def in_blocks(x, dim, peers):
    before, after = (x.shape[:dim], x.shape[dim + 1 :])
    return jnp.moveaxis(x.reshape(*before, peers, -1, *after), dim, 0)


def sent_and_summed(x, axis, dim):
    peers = lax.axis_size(axis)
    parts = lax.all_to_all(in_blocks(x, dim, peers), axis, 0, 0, tiled=True)
    return jnp.sum(parts, axis=0)


def spread(shard, slots):
    experts, rows_shard, width = shard.shape
    places = lax.axis_size("place")
    select = (slots[:, None] == jnp.arange(experts, dtype=jnp.int32)[None, :]).astype(jnp.bfloat16)
    picked = jnp.dot(
        select, shard.reshape(experts, rows_shard * width), preferred_element_type=jnp.float32
    ).astype(jnp.bfloat16)
    landed = lax.all_to_all(
        picked.reshape(places, rows_shard, width), "place", split_axis=0, concat_axis=0, tiled=True
    )
    whole = gathered_copies(landed.reshape(places * rows_shard, width), "dp", 0)
    return whole


def batch_grad(total, rows_in, grads_in, order, count, weights, start):
    rows = order.shape[0]
    half = weights.shape[1] // 2
    picked = jnp.take(rows_in, start + order, axis=0)
    both = jnp.dot(picked, weights, preferred_element_type=jnp.float32)
    gate = both[:, :half]
    upward = both[:, half:]
    sigma = jax.nn.sigmoid(gate)
    active = gate * sigma
    slope = sigma * (1.0 + gate * (1.0 - sigma))
    live = start + jnp.arange(rows, dtype=jnp.int32) < count
    incoming = jnp.where(live[:, None], grads_in[start : start + rows].astype(jnp.float32), 0.0)
    local = jnp.concatenate([incoming * upward * slope, incoming * active], axis=1).astype(
        jnp.bfloat16
    )
    return total + lax.dot_general(
        picked, local, (((0,), (0,)), ((), ())), preferred_element_type=jnp.float32
    )


def shards(
    tokens,
    hidden_grad,
    routing,
    row_count,
    old_slots,
    new_slots,
    master,
    first_moment,
    second_moment,
):
    places = lax.axis_size("place")
    groups = lax.axis_size("dp")
    experts, rows_shard, width = master.shape
    place_here = lax.axis_index("place")
    group_here = lax.axis_index("dp")
    weights = spread(master.astype(jnp.bfloat16), old_slots)
    rows_in = tokens[0, 0]
    grads_in = hidden_grad[0, 0]
    order = routing[0, 0]
    count = row_count[group_here, place_here]
    batch_rows = order.shape[1]
    summed = jnp.zeros((rows_in.shape[1], width), jnp.float32)
    for batch_index in range(order.shape[0]):
        start = batch_index * batch_rows
        summed = batch_grad(summed, rows_in, grads_in, order[batch_index], count, weights, start)
    select = (old_slots[:, None] == jnp.arange(experts, dtype=jnp.int32)[None, :]).astype(
        jnp.float32
    )
    blocks = summed.reshape(groups, places, rows_shard, width)
    partial_sum = sent_and_summed(blocks, "dp", 0)
    landed = lax.all_to_all(partial_sum, "place", split_axis=1, concat_axis=1, tiled=True)
    grad_sum = jnp.dot(
        select.T, landed.reshape(places, rows_shard * width), precision=lax.Precision.HIGHEST
    ).reshape(experts, rows_shard, width)
    per_slot = jnp.sum(row_count.astype(jnp.float32), axis=0)
    total = jnp.dot(per_slot, select, precision=lax.Precision.HIGHEST)
    grad = grad_sum / total[:, None, None]
    new_first = decay_first * first_moment + (1.0 - decay_first) * grad
    new_second = decay_second * second_moment + (1.0 - decay_second) * grad * grad
    first_hat = new_first / (1.0 - decay_first**step_number)
    second_hat = new_second / (1.0 - decay_second**step_number)
    new_master = master - learn_rate * (
        first_hat / (jnp.sqrt(second_hat) + epsilon) + weight_decay * master
    )
    new_weights = spread(new_master.astype(jnp.bfloat16), new_slots)
    return (new_weights[None], new_master, new_first, new_second)


def solution(mesh):
    placed = (
        P("dp", "place", None, None),
        P("dp", "place", None, None),
        P("dp", "place", None, None),
        P(),
        P(),
        P(),
        P(None, ("dp", "place"), None),
        P(None, ("dp", "place"), None),
        P(None, ("dp", "place"), None),
    )
    return jax.shard_map(
        shards,
        mesh=mesh,
        in_specs=placed,
        out_specs=(
            P("place", None, None),
            P(None, ("dp", "place"), None),
            P(None, ("dp", "place"), None),
            P(None, ("dp", "place"), None),
        ),
        check_vma=False,
    )
```

profile of v0, /device:TPU:1, one launch (start us, length us, event | category | flops | bytes accessed | tf_op | source)
XLA Modules:
  0.0 247.8 jit_solution(2621490347751096984)
XLA Ops:
  0.6 1.0 convert_element_type.48
  1.7 0.9 convolution_convert_fusion.1
  2.8 38.0 %all_to_all.30 = bf16[64,4,512]{2,1,0:T(4,128)(2,1)S(1)} all-to-all(bf16[64,4,512]{2,1,0:T(4,128)(2,1)S(1)} %reshape.89), channel_id=1, replica_groups=mesh['dp'=8,'place'=64] {'place'}, dimensions={0} | all-to-all | bytes 524288 | tf_op jit(solution)/shard_map/all_to_all | solution.py:48
  40.9 1.5 broadcast_in_dim.58
  42.4 7.5 %all-to-all-start.1 = ((bf16[8,256,512]{2,1,0:T(8,128)(2,1)}), bf16[8,256,512]{2,1,0:T(8,128)(2,1)S(1)}, u32[]{:S(2)}, u32[]{:S(2)}) async-start(bf16[8,256,512]{2,1,0:T(8,128)(2,1)} %broadcast_in_dim.58), calls=%async_computation.1 | async-start | bytes 4194304 | tf_op jit(solution)/shard_map/all_to_all | solution.py:16
  49.9 1.4 gather_fusion
  51.3 1.4 gather_fusion.1
  53.5 1.4 gather_fusion.2
  56.9 19.2 %all-to-all-done.1 = bf16[8,256,512]{2,1,0:T(8,128)(2,1)S(1)} async-done(((bf16[8,256,512]{2,1,0:T(8,128)(2,1)}), bf16[8,256,512]{2,1,0:T(8,128)(2,1)S(1)}, u32[]{:S(2)}, u32[]{:S(2)}) %all-to-all-start.1) | async-done | bytes 2097184 | tf_op jit(solution)/shard_map/all_to_all | solution.py:16
  76.0 1.5 fusion.5
  78.8 0.8 fusion.6
  79.7 0.8 fusion.4
  81.3 0.8 fusion.8
  82.1 2.8 %add_add_fusion = f32[2048,512]{1,0:T(8,128)} fusion(f32[2048,512]{1,0:T(8,128)S(1)} %fusion.8, f32[2048,512]{1,0:T(8,128)S(1)} %fusion.4, f32[2048,512]{1,0:T(8,128)S(1)} %fusion.6, bf16[64,2048]{1,0:T(8,128)(2,1)S(1)} %gather_fusion.3, pred[64]{0:T(512)(128)(4,1)S(1)} %get-tuple-element.21, bf16[64,256]{1,0:T(8,128)(2,1)S(1)} %get-tuple-element.30, ...), kind=kOutput, calls=%fused_computation.4 | convolution fusion | flops 137625600 | bytes 17104960 | tf_op jit(solution)/shard_map/dot_general | solution.py:70
  84.9 5.2 %reshape_reshape.3 = f32[8,1,64,4,512]{4,3,2,0,1:T(4,128)} reshape(f32[2048,512]{1,0:T(8,128)} %add_add_fusion) | data formatting | bytes 8388608 | tf_op jit(solution)/shard_map/reshape;reshape | solution.py:32
  90.1 54.1 %all_to_all.31 = f32[8,1,64,4,512]{4,3,2,1,0:T(4,128)} all-to-all(f32[8,1,64,4,512]{4,3,2,1,0:T(4,128)} %bitcast.78), channel_id=1, replica_groups=mesh['dp'=8,'place'=64] {'dp'}, dimensions={0} | all-to-all | bytes 8388608 | tf_op jit(solution)/shard_map/all_to_all | solution.py:37
  144.2 3.9 %reduce_sum.20 = f32[64,4,512]{2,1,0:T(4,128)} reduce(f32[8,1,64,4,512]{4,3,2,1,0:T(4,128)} %all_to_all.31, f32[]{:T(128)} %constant.16.clone.1), dimensions={0,1}, to_apply=%region_0.0 | reduce | flops 917504 | bytes 4718596 | tf_op jit(solution)/shard_map/reduce_sum | solution.py:38
  148.1 6.3 %all-to-all-start.3 = ((f32[1,64,4,512]{3,2,0,1:T(4,128)}), f32[1,64,4,512]{3,2,0,1:T(4,128)S(1)}, u32[]{:S(2)}, u32[]{:S(2)}) async-start(f32[1,64,4,512]{3,2,0,1:T(4,128)} %bitcast.13), calls=%async_computation.3 | async-start | bytes 1048576 | tf_op jit(solution)/shard_map/all_to_all | solution.py:106
  154.5 29.2 %all-to-all-done.3 = f32[1,64,4,512]{3,2,0,1:T(4,128)S(1)} async-done(((f32[1,64,4,512]{3,2,0,1:T(4,128)}), f32[1,64,4,512]{3,2,0,1:T(4,128)S(1)}, u32[]{:S(2)}, u32[]{:S(2)}) %all-to-all-start.3) | async-done | bytes 524320 | tf_op jit(solution)/shard_map/all_to_all | solution.py:106
  184.8 27.1 %all_to_all.32 = bf16[64,4,512]{2,1,0:T(4,128)(2,1)S(1)} all-to-all(bf16[64,4,512]{2,1,0:T(4,128)(2,1)S(1)} %reshape.94), channel_id=1, replica_groups=mesh['dp'=8,'place'=64] {'place'}, dimensions={0} | all-to-all | bytes 524288 | tf_op jit(solution)/shard_map/all_to_all | solution.py:48
  212.0 1.5 broadcast_in_dim.62
  213.5 6.7 %all-to-all-start.5 = ((bf16[8,256,512]{2,1,0:T(8,128)(2,1)}), bf16[8,256,512]{2,1,0:T(8,128)(2,1)S(1)}, u32[]{:S(2)}, u32[]{:S(2)}) async-start(bf16[8,256,512]{2,1,0:T(8,128)(2,1)} %broadcast_in_dim.62), calls=%async_computation.5 | async-start | bytes 4194304 | tf_op jit(solution)/shard_map/all_to_all | solution.py:16
  222.5 24.0 %all-to-all-done.5 = bf16[8,256,512]{2,1,0:T(8,128)(2,1)S(1)} async-done(((bf16[8,256,512]{2,1,0:T(8,128)(2,1)}), bf16[8,256,512]{2,1,0:T(8,128)(2,1)S(1)}, u32[]{:S(2)}, u32[]{:S(2)}) %all-to-all-start.5) | async-done | bytes 2097184 | tf_op jit(solution)/shard_map/all_to_all | solution.py:16
  246.5 1.3 copy.63
  (49 shorter events, 8.4 us)
Async XLA Ops:
  0.6 49.2 %copy-start = (bf16[1,1,256,2048]{3,2,1,0:T(8,128)(2,1)S(1)}, bf16[1,1,256,2048]{3,2,1,0:T(8,128)(2,1)}, u32[]{:S(2)}) copy-start(bf16[1,1,256,2048]{3,2,1,0:T(8,128)(2,1)} %param.11) | copy-start | bytes 3145732
  42.4 7.5 %copy-start.7 = (s32[1,1,4,64]{3,2,1,0:T(4,128)S(1)}, s32[1,1,4,64]{3,2,1,0:T(4,128)}, u32[]{:S(2)}) copy-start(s32[1,1,4,64]{3,2,1,0:T(4,128)} %param.13) | copy-start | bytes 3076
  42.4 33.7 %all-to-all-start.1 = ((bf16[8,256,512]{2,1,0:T(8,128)(2,1)}), bf16[8,256,512]{2,1,0:T(8,128)(2,1)S(1)}, u32[]{:S(2)}, u32[]{:S(2)}) async-start(bf16[8,256,512]{2,1,0:T(8,128)(2,1)} %broadcast_in_dim.58), calls=%async_computation.1 | async-start | bytes 4194304 | tf_op jit(solution)/shard_map/all_to_all | solution.py:16
  52.8 2.2 copy-start.6
  76.0 1.5 copy-start.2
  77.6 1.1 copy-start.4
  78.8 1.0 copy-start.1
  79.7 0.9 copy-start.3
  144.2 10.2 %copy-start.8 = (s32[64]{0:T(128)S(1)}, s32[64]{0:T(128)}, u32[]{:S(2)}) copy-start(s32[64]{0:T(128)} %param.15) | copy-start | bytes 772
  144.2 39.5 %copy-start.5 = (f32[16,4,512]{2,1,0:T(4,128)S(1)}, f32[16,4,512]{2,1,0:T(4,128)}, u32[]{:S(2)}) copy-start(f32[16,4,512]{2,1,0:T(4,128)} %param.17) | copy-start | bytes 393220
  144.2 39.5 %copy-start.10 = (f32[16,4,512]{2,1,0:T(4,128)S(1)}, f32[16,4,512]{2,1,0:T(4,128)}, u32[]{:S(2)}) copy-start(f32[16,4,512]{2,1,0:T(4,128)} %param.18) | copy-start | bytes 393220
  144.2 39.5 %copy-start.11 = (f32[16,4,512]{2,1,0:T(4,128)S(1)}, f32[16,4,512]{2,1,0:T(4,128)}, u32[]{:S(2)}) copy-start(f32[16,4,512]{2,1,0:T(4,128)} %param.19) | copy-start | bytes 393220
  148.1 36.2 %copy-start.9 = (s32[64]{0:T(128)S(1)}, s32[64]{0:T(128)}, u32[]{:S(2)}) copy-start(s32[64]{0:T(128)} %param.16) | copy-start | bytes 772
  148.1 35.6 %all-to-all-start.3 = ((f32[1,64,4,512]{3,2,0,1:T(4,128)}), f32[1,64,4,512]{3,2,0,1:T(4,128)S(1)}, u32[]{:S(2)}, u32[]{:S(2)}) async-start(f32[1,64,4,512]{3,2,0,1:T(4,128)} %bitcast.13), calls=%async_computation.3 | async-start | bytes 1048576 | tf_op jit(solution)/shard_map/all_to_all | solution.py:106
  213.5 33.0 %all-to-all-start.5 = ((bf16[8,256,512]{2,1,0:T(8,128)(2,1)}), bf16[8,256,512]{2,1,0:T(8,128)(2,1)S(1)}, u32[]{:S(2)}, u32[]{:S(2)}) async-start(bf16[8,256,512]{2,1,0:T(8,128)(2,1)} %broadcast_in_dim.62), calls=%async_computation.5 | async-start | bytes 4194304 | tf_op jit(solution)/shard_map/all_to_all | solution.py:16
where the time goes:
time: 248 us
  blocking collectives  119 us (48%)
  waiting for transfers between devices  72.4 us (29%)
  starting transfers between devices  20.5 us (8%)
  local copies, waits for them, and re-layouts  18.2 us (7%)
  matrix products  10.2 us (4%)
  other arithmetic  6.47 us (3%)
    all_to_all x2, blocking collectives, spread(): lax.all_to_all(picked.reshape(places, rows_shard, width), 'place', split_...  65.1 us
    all_to_all x1, blocking collectives, sent_and_summed(): parts = lax.all_to_all(in_blocks(x, dim, peers), axis, 0, 0, tiled=True)  54.1 us
    all_to_all x2, waiting for transfers between devices, from_everyone(): return lax.all_to_all(copies, axis, split_axis=0, concat_axis=0, tiled=True)  43.2 us
    all_to_all x1, waiting for transfers between devices, shards(): lax.all_to_all(partial_sum, 'place', split_axis=1, concat_axis=1, tiled=T...  29.2 us
    all_to_all x2, starting transfers between devices, from_everyone(): return lax.all_to_all(copies, axis, split_axis=0, concat_axis=0, tiled=True)  14.2 us
    all_to_all x1, starting transfers between devices, shards(): lax.all_to_all(partial_sum, 'place', split_axis=1, concat_axis=1, tiled=T...  6.27 us
    dot_general x4, matrix products, batch_grad(): lax.dot_general(picked, local, (((0,), (0,)), ((), ())), preferred_elemen...  5.23 us
    another operation x1, local copies, waits for them, and re-layouts, in_blocks(): return jnp.moveaxis(x.reshape(*before, peers, -1, *after), dim, 0)  5.18 us
  transfers between devices with their start and end apart: 3, of which 3 were waited for; matrix products, arithmetic and copies ran while one was open for 4% of the time, Pallas kernels for 0%

commit v1 on v0

--- a/solution.py
+++ b/solution.py
@@ -103,7 +103,12 @@
     )
     blocks = summed.reshape(groups, places, rows_shard, width)
     partial_sum = sent_and_summed(blocks, "dp", 0)
-    landed = lax.all_to_all(partial_sum, "place", split_axis=1, concat_axis=1, tiled=True)
+    landed = jnp.concatenate(
+        lax.all_to_all(
+            jnp.stack(jnp.split(partial_sum, lax.axis_size("place"), axis=1)), "place", 0, 0
+        ),
+        axis=1,
+    )
     grad_sum = jnp.dot(
         select.T, landed.reshape(places, rows_shard * width), precision=lax.Precision.HIGHEST
     ).reshape(experts, rows_shard, width)

time: 248 us -> 286 us (1.15)
  local copies, waits for them, and re-layouts: 18.2 us -> 56.6 us
    unnamed x29 -> x92, local copies, waits for them, and re-layouts: 3.87 us -> 41.6 us
  transfers between devices with their start and end apart: 3 -> 3, of which waited for: 3 -> 3; matrix products, arithmetic and copies ran while one was open for 4% -> 3% of each run, Pallas kernels for 0% -> 0%
where the time goes in v1:
time: 286 us; the launch traced here: 285 us
  blocking collectives  119 us (42%)
  waiting for transfers between devices  72.4 us (25%)
  local copies, waits for them, and re-layouts  56.6 us (20%)
  starting transfers between devices  20.3 us (7%)
  matrix products  10.2 us (4%)
  other arithmetic  5.56 us (2%)
    all_to_all x2, blocking collectives, spread(): lax.all_to_all(picked.reshape(places, rows_shard, width), 'place', split_...  65.1 us
    all_to_all x1, blocking collectives, sent_and_summed(): parts = lax.all_to_all(in_blocks(x, dim, peers), axis, 0, 0, tiled=True)  54.1 us
    all_to_all x2, waiting for transfers between devices, from_everyone(): return lax.all_to_all(copies, axis, split_axis=0, concat_axis=0, tiled=True)  43.2 us
    unnamed x92, local copies, waits for them, and re-layouts  41.6 us
    all_to_all x1, waiting for transfers between devices, shards(): lax.all_to_all(jnp.stack(jnp.split(partial_sum, lax.axis_size('place'), a...  29.2 us
    all_to_all x2, starting transfers between devices, from_everyone(): return lax.all_to_all(copies, axis, split_axis=0, concat_axis=0, tiled=True)  14.2 us
    all_to_all x1, starting transfers between devices, shards(): lax.all_to_all(jnp.stack(jnp.split(partial_sum, lax.axis_size('place'), a...  6.14 us
  transfers between devices with their start and end apart: 3, of which 3 were waited for; matrix products, arithmetic and copies ran while one was open for 3% of the time, Pallas kernels for 0%

profile of v1, /device:TPU:1, one launch (start us, length us, event | category | flops | bytes accessed | tf_op | source)
XLA Modules:
  0.0 285.2 jit_solution(11843191302656856019)
XLA Ops:
  0.6 1.0 convert_element_type.48
  1.7 0.9 convolution_convert_fusion.1
  2.8 38.0 %all_to_all.30 = bf16[64,4,512]{2,1,0:T(4,128)(2,1)S(1)} all-to-all(bf16[64,4,512]{2,1,0:T(4,128)(2,1)S(1)} %reshape.86), channel_id=1, replica_groups=mesh['dp'=8,'place'=64] {'place'}, dimensions={0} | all-to-all | bytes 524288 | tf_op jit(solution)/shard_map/all_to_all | solution.py:48
  40.9 1.5 broadcast_in_dim.58
  42.4 7.5 %all-to-all-start.1 = ((bf16[8,256,512]{2,1,0:T(8,128)(2,1)}), bf16[8,256,512]{2,1,0:T(8,128)(2,1)S(1)}, u32[]{:S(2)}, u32[]{:S(2)}) async-start(bf16[8,256,512]{2,1,0:T(8,128)(2,1)} %broadcast_in_dim.58), calls=%async_computation.1 | async-start | bytes 4194304 | tf_op jit(solution)/shard_map/all_to_all | solution.py:16
  49.9 1.4 gather_fusion
  51.3 1.4 gather_fusion.1
  53.5 1.4 gather_fusion.2
  56.9 19.2 %all-to-all-done.1 = bf16[8,256,512]{2,1,0:T(8,128)(2,1)S(1)} async-done(((bf16[8,256,512]{2,1,0:T(8,128)(2,1)}), bf16[8,256,512]{2,1,0:T(8,128)(2,1)S(1)}, u32[]{:S(2)}, u32[]{:S(2)}) %all-to-all-start.1) | async-done | bytes 2097184 | tf_op jit(solution)/shard_map/all_to_all | solution.py:16
  76.0 1.5 fusion.5
  78.8 0.8 fusion.6
  79.7 0.8 fusion.4
  81.3 0.8 fusion.8
  82.1 2.8 add_add_fusion
  84.9 5.2 %reshape_reshape.6 = f32[8,1,64,4,512]{4,3,2,0,1:T(4,128)} reshape(f32[2048,512]{1,0:T(8,128)} %add_add_fusion) | data formatting | bytes 8388608 | tf_op jit(solution)/shard_map/reshape;reshape | solution.py:32
  90.1 54.1 %all_to_all.31 = f32[8,1,64,4,512]{4,3,2,1,0:T(4,128)} all-to-all(f32[8,1,64,4,512]{4,3,2,1,0:T(4,128)} %bitcast.333), channel_id=1, replica_groups=mesh['dp'=8,'place'=64] {'dp'}, dimensions={0} | all-to-all | bytes 8388608 | tf_op jit(solution)/shard_map/all_to_all | solution.py:37
  144.2 3.0 %reduce_sum.20 = f32[64,4,512]{2,1,0:T(4,128)S(1)} reduce(f32[8,1,64,4,512]{4,3,2,1,0:T(4,128)} %all_to_all.31, f32[]{:T(128)} %constant.16.clone.1), dimensions={0,1}, to_apply=%region_0.0 | reduce | flops 917504 | bytes 4718596 | tf_op jit(solution)/shard_map/reduce_sum | solution.py:38
  185.6 6.1 %all-to-all-start.3 = ((f32[64,1,1,4,512]{4,3,2,1,0:T(4,128)}), f32[64,1,1,4,512]{4,3,2,1,0:T(4,128)S(1)}, u32[]{:S(2)}, u32[]{:S(2)}) async-start(f32[64,1,1,4,512]{4,3,2,1,0:T(4,128)} %constant_dynamic-update-slice_fusion), calls=%async_computation.3 | async-start | bytes 1048576 | tf_op jit(solution)/shard_map/all_to_all | solution.py:107
  191.9 29.2 %all-to-all-done.3 = f32[64,1,1,4,512]{4,3,2,1,0:T(4,128)S(1)} async-done(((f32[64,1,1,4,512]{4,3,2,1,0:T(4,128)}), f32[64,1,1,4,512]{4,3,2,1,0:T(4,128)S(1)}, u32[]{:S(2)}, u32[]{:S(2)}) %all-to-all-start.3) | async-done | bytes 524320 | tf_op jit(solution)/shard_map/all_to_all | solution.py:107
  222.1 27.1 %all_to_all.32 = bf16[64,4,512]{2,1,0:T(4,128)(2,1)S(1)} all-to-all(bf16[64,4,512]{2,1,0:T(4,128)(2,1)S(1)} %reshape.90), channel_id=1, replica_groups=mesh['dp'=8,'place'=64] {'place'}, dimensions={0} | all-to-all | bytes 524288 | tf_op jit(solution)/shard_map/all_to_all | solution.py:48
  249.4 1.5 broadcast_in_dim.62
  250.9 6.7 %all-to-all-start.5 = ((bf16[8,256,512]{2,1,0:T(8,128)(2,1)}), bf16[8,256,512]{2,1,0:T(8,128)(2,1)S(1)}, u32[]{:S(2)}, u32[]{:S(2)}) async-start(bf16[8,256,512]{2,1,0:T(8,128)(2,1)} %broadcast_in_dim.62), calls=%async_computation.5 | async-start | bytes 4194304 | tf_op jit(solution)/shard_map/all_to_all | solution.py:16
  259.8 24.0 %all-to-all-done.5 = bf16[8,256,512]{2,1,0:T(8,128)(2,1)S(1)} async-done(((bf16[8,256,512]{2,1,0:T(8,128)(2,1)}), bf16[8,256,512]{2,1,0:T(8,128)(2,1)S(1)}, u32[]{:S(2)}, u32[]{:S(2)}) %all-to-all-start.5) | async-done | bytes 2097184 | tf_op jit(solution)/shard_map/all_to_all | solution.py:16
  283.8 1.3 copy.189
  (113 shorter events, 46.8 us)
Async XLA Ops:
  0.6 49.2 %copy-start = (bf16[1,1,256,2048]{3,2,1,0:T(8,128)(2,1)S(1)}, bf16[1,1,256,2048]{3,2,1,0:T(8,128)(2,1)}, u32[]{:S(2)}) copy-start(bf16[1,1,256,2048]{3,2,1,0:T(8,128)(2,1)} %param.11) | copy-start | bytes 3145732
  42.4 7.5 %copy-start.7 = (s32[1,1,4,64]{3,2,1,0:T(4,128)S(1)}, s32[1,1,4,64]{3,2,1,0:T(4,128)}, u32[]{:S(2)}) copy-start(s32[1,1,4,64]{3,2,1,0:T(4,128)} %param.13) | copy-start | bytes 3076
  42.4 33.7 %all-to-all-start.1 = ((bf16[8,256,512]{2,1,0:T(8,128)(2,1)}), bf16[8,256,512]{2,1,0:T(8,128)(2,1)S(1)}, u32[]{:S(2)}, u32[]{:S(2)}) async-start(bf16[8,256,512]{2,1,0:T(8,128)(2,1)} %broadcast_in_dim.58), calls=%async_computation.1 | async-start | bytes 4194304 | tf_op jit(solution)/shard_map/all_to_all | solution.py:16
  52.8 2.2 copy-start.6
  76.0 1.5 copy-start.2
  77.6 1.1 copy-start.4
  78.8 1.0 copy-start.1
  79.7 0.9 copy-start.3
  147.2 44.6 %copy-start.8 = (s32[64]{0:T(128)S(1)}, s32[64]{0:T(128)}, u32[]{:S(2)}) copy-start(s32[64]{0:T(128)} %param.15) | copy-start | bytes 772
  147.2 73.9 %copy-start.5 = (f32[16,4,512]{2,1,0:T(4,128)S(1)}, f32[16,4,512]{2,1,0:T(4,128)}, u32[]{:S(2)}) copy-start(f32[16,4,512]{2,1,0:T(4,128)} %param.17) | copy-start | bytes 393220
  147.2 73.9 %copy-start.10 = (f32[16,4,512]{2,1,0:T(4,128)S(1)}, f32[16,4,512]{2,1,0:T(4,128)}, u32[]{:S(2)}) copy-start(f32[16,4,512]{2,1,0:T(4,128)} %param.18) | copy-start | bytes 393220
  147.2 73.9 %copy-start.11 = (f32[16,4,512]{2,1,0:T(4,128)S(1)}, f32[16,4,512]{2,1,0:T(4,128)}, u32[]{:S(2)}) copy-start(f32[16,4,512]{2,1,0:T(4,128)} %param.19) | copy-start | bytes 393220
  147.2 74.5 %copy-start.9 = (s32[64]{0:T(128)S(1)}, s32[64]{0:T(128)}, u32[]{:S(2)}) copy-start(s32[64]{0:T(128)} %param.16) | copy-start | bytes 772
  185.6 35.5 %all-to-all-start.3 = ((f32[64,1,1,4,512]{4,3,2,1,0:T(4,128)}), f32[64,1,1,4,512]{4,3,2,1,0:T(4,128)S(1)}, u32[]{:S(2)}, u32[]{:S(2)}) async-start(f32[64,1,1,4,512]{4,3,2,1,0:T(4,128)} %constant_dynamic-update-slice_fusion), calls=%async_computation.3 | async-start | bytes 1048576 | tf_op jit(solution)/shard_map/all_to_all | solution.py:107
  250.9 33.0 %all-to-all-start.5 = ((bf16[8,256,512]{2,1,0:T(8,128)(2,1)}), bf16[8,256,512]{2,1,0:T(8,128)(2,1)S(1)}, u32[]{:S(2)}, u32[]{:S(2)}) async-start(bf16[8,256,512]{2,1,0:T(8,128)(2,1)} %broadcast_in_dim.62), calls=%async_computation.5 | async-start | bytes 4194304 | tf_op jit(solution)/shard_map/all_to_all | solution.py:16
